TPU v7x, 256 devices: a whole 4x4x8 slice. The times are simulated.
256 devices in a mesh: band: 8 (over z_lo, core), span: 32 (over x, y, z_hi).
Axes of the slice: x: 4, y: 4, z: 8 (z_hi: 2, z_lo: 4; z = z_hi * 4 + z_lo), core: 2. Of those that a mesh axis runs over, the one named last changes fastest.
Arguments:
- gases: bfloat16 [7, 32, 131072], P(None, None, ('band', 'span')), may hold values from 0 to 1
- pressure_bin: int32 [32, 131072], P(None, ('band', 'span')), may hold values from 0 to 59
- layer_mass: bfloat16 [32, 131072], P(None, ('band', 'span')), may hold values from 0.5 to 2
- cos_zenith: bfloat16 [131072], P(('band', 'span')), may hold values from 0.19921875 to 1
- surface_albedo: bfloat16 [131072], P(('band', 'span')), may hold values from 0.049804688 to 0.8984375
- column_order: int32 [131072], P(('band', 'span')), may hold values from 0 to 511, as said below
- sunlit: int32 [1024], P(('band', 'span')), may hold values from 0 to 1, as said below
- absorption: bfloat16 [112, 7, 60], replicated, may hold values from 9.9658966e-05 to 0.099609375
- scattering: bfloat16 [112, 60], replicated, may hold values from 0.19921875 to 0.94921875
Outputs:
- heating: float32 [32, 131072], P(None, ('band', 'span'))
Inputs may be any that keep to these rules, and one draw needn't show every extreme that they name: `column_order`: the 512 entries of each device's slice are a permutation of 0 to 511. The 8 devices with the same index along the second mesh axis hold 16 sunlit blocks together; among them one device has all 4 blocks sunlit and one has none.
All inputs are finite; a program needn't handle non-finite values.
Results may differ from a plain program's by a relative error of at most 0.0003.
Values may be sent and summed in bfloat16 or wider, within the bound.
A program may use at most 64 MiB of HBM per device.

v0:
```python
import jax
import jax.numpy as jnp
from jax import lax
from jax.sharding import PartitionSpec as P


def column_heating(profile, ground_pair, absorption, scattering):
    gas_count = absorption.shape[1]
    bin_count = scattering.shape[1]
    levels = profile.shape[1]
    col_count = profile.shape[2]
    groups = levels // 8
    amounts = profile[:gas_count]
    bin_index = profile[gas_count].astype(jnp.int32)
    thickness = profile[gas_count + 1].astype(jnp.float32)
    cosine = ground_pair[0, 0].astype(jnp.float32)
    ground = ground_pair[1, 0].astype(jnp.float32)
    selector = (
        bin_index[None] == lax.broadcasted_iota(jnp.int32, (bin_count, levels, col_count), 0)
    ).astype(jnp.bfloat16)
    weighted = (amounts[:, None] * selector[None]).reshape(gas_count * bin_count, levels, col_count)
    table = absorption.reshape(absorption.shape[0], gas_count * bin_count)
    optical_depth = jnp.einsum("gk,kln->lgn", table, weighted, preferred_element_type=jnp.float32)
    albedo = jnp.einsum("gk,kln->lgn", scattering, selector, preferred_element_type=jnp.float32)
    column_path = jnp.cumsum(optical_depth, axis=0)
    column_path = jnp.concatenate([jnp.zeros_like(column_path[:1]), column_path], axis=0)
    direct = cosine * jnp.exp(-column_path / cosine)
    fading = jnp.exp(-1.66 * optical_depth)
    reflect = 0.5 * albedo * (1.0 - fading)
    transmit = fading + reflect
    source = 0.5 * albedo * (direct[:-1] - direct[1:])
    grouped_shape = (groups, 8) + reflect.shape[1:]

    def upward(state_pair, layer):
        refl_below, source_below = state_pair
        layer_reflect, layer_transmit, layer_source = layer
        refl_rows = []
        source_rows = []
        for offset in range(7, -1, -1):
            denominator = 1.0 - layer_reflect[offset] * refl_below
            refl_next = (
                layer_reflect[offset]
                + layer_transmit[offset] * layer_transmit[offset] * refl_below / denominator
            )
            source_below = (
                layer_source[offset]
                + layer_transmit[offset]
                * (source_below + refl_below * layer_source[offset])
                / denominator
            )
            refl_below = refl_next
            refl_rows.insert(0, refl_below)
            source_rows.insert(0, source_below)
        return ((refl_below, source_below), (jnp.stack(refl_rows), jnp.stack(source_rows)))

    floor_refl = jnp.broadcast_to(ground, reflect.shape[1:])
    floor_source = ground * direct[-1]
    final_pair, tops = lax.scan(
        upward,
        (floor_refl, floor_source),
        (
            reflect.reshape(grouped_shape),
            transmit.reshape(grouped_shape),
            source.reshape(grouped_shape),
        ),
        reverse=True,
    )
    refl_all = jnp.concatenate([tops[0].reshape(reflect.shape), floor_refl[None]], axis=0)
    source_all = jnp.concatenate([tops[1].reshape(reflect.shape), floor_source[None]], axis=0)

    def downward(diffuse, layer):
        layer_reflect, layer_transmit, layer_source, refl_low, source_low = layer
        level_rows = []
        for offset in range(8):
            denominator = 1.0 - layer_reflect[offset] * refl_low[offset]
            diffuse = (
                layer_transmit[offset] * diffuse
                + layer_reflect[offset] * source_low[offset]
                + layer_source[offset]
            ) / denominator
            level_rows.append(diffuse)
        return (diffuse, jnp.stack(level_rows))

    start_diffuse = jnp.zeros_like(floor_refl)
    final_diffuse, lower = lax.scan(
        downward,
        start_diffuse,
        (
            reflect.reshape(grouped_shape),
            transmit.reshape(grouped_shape),
            source.reshape(grouped_shape),
            refl_all[1:].reshape(grouped_shape),
            source_all[1:].reshape(grouped_shape),
        ),
    )
    diffuse_all = jnp.concatenate([start_diffuse[None], lower.reshape(reflect.shape)], axis=0)
    net = direct + diffuse_all - (refl_all * diffuse_all + source_all)
    return jnp.sum(net[:-1] - net[1:], axis=1) / thickness


def blocks_heating(field_blocks, ground_blocks, absorption, scattering):
    moved_fields = jnp.moveaxis(field_blocks, 2, 0)
    moved_ground = jnp.moveaxis(ground_blocks, 2, 0)
    result = lax.map(
        lambda inputs_pair: column_heating(inputs_pair[0], inputs_pair[1], absorption, scattering),
        (moved_fields, moved_ground),
    )
    return jnp.moveaxis(result, 0, 1)


def local(
    gases,
    pressure_bin,
    layer_mass,
    cos_zenith,
    surface_albedo,
    column_order,
    sunlit,
    absorption,
    scattering,
):
    band_count = lax.axis_size("band")
    group_size = lax.axis_size("span")
    me_band = lax.axis_index("band")
    columns = column_order.shape[0]
    per_peer = columns // group_size
    block_count = sunlit.shape[0]
    block_cols = columns // block_count
    levels = layer_mass.shape[0]
    fields = jnp.concatenate(
        [gases, pressure_bin.astype(jnp.bfloat16)[None], layer_mass[None]], axis=0
    )
    field_rows = fields.shape[0]
    ground = jnp.stack([cos_zenith, surface_albedo])[:, None]
    ordering = column_order.reshape(group_size, per_peer)
    fields = jnp.take(fields, ordering, axis=2)
    ground = jnp.take(ground, ordering, axis=2)
    fields, ground = (
        lax.all_to_all(fields, "span", split_axis=2, concat_axis=2, tiled=True),
        lax.all_to_all(ground, "span", split_axis=2, concat_axis=2, tiled=True),
    )
    fields = fields.reshape(field_rows, levels, block_count, block_cols)
    ground = ground.reshape(2, 1, block_count, block_cols)
    flag_mask = sunlit.astype(jnp.float32)[:, None]
    flag_table = lax.all_gather(sunlit, "band", axis=0, tiled=True).reshape(band_count, block_count)
    counts = jnp.sum(flag_table, axis=1)
    band_ends = jnp.cumsum(counts)
    starts = band_ends - counts
    own_start = starts[me_band]
    own_rank = jnp.cumsum(sunlit) - sunlit
    slot_count = -(-block_count // band_count)
    working = block_count // 2
    target = jnp.arange(band_count, dtype=jnp.int32)[:, None]
    position = jnp.arange(slot_count, dtype=jnp.int32)[None, :]
    wanted = position * band_count + (target - own_start) % band_count
    matches = (sunlit[None, None, :] == 1) & (own_rank[None, None, :] == wanted[:, :, None])
    chosen = jnp.sum(
        jnp.where(matches, jnp.arange(block_count, dtype=jnp.int32), 0), axis=2
    ).reshape(-1)
    send_fields = jnp.take(fields, chosen, axis=2).reshape(
        field_rows, levels, band_count, slot_count, block_cols
    )
    send_ground = jnp.take(ground, chosen, axis=2).reshape(2, 1, band_count, slot_count, block_cols)
    got_fields, got_ground = (
        lax.all_to_all(send_fields, "band", split_axis=2, concat_axis=2, tiled=True),
        lax.all_to_all(send_ground, "band", split_axis=2, concat_axis=2, tiled=True),
    )
    work_rank = jnp.arange(working, dtype=jnp.int32) * band_count + me_band
    source_band = jnp.sum((band_ends[None, :] <= work_rank[:, None]).astype(jnp.int32), axis=1)
    within = work_rank - starts[source_band]
    work_pick = source_band * slot_count + within // band_count
    work_fields = jnp.take(
        got_fields.reshape(field_rows, levels, band_count * slot_count, block_cols),
        work_pick,
        axis=2,
    )
    work_ground = jnp.take(
        got_ground.reshape(2, 1, band_count * slot_count, block_cols), work_pick, axis=2
    )
    heating = blocks_heating(work_fields, work_ground, absorption, scattering)
    inner_back = position * band_count + (me_band - starts[:, None]) % band_count
    rank_back = starts[:, None] + inner_back
    slot_back = jnp.clip(rank_back // band_count, 0, working - 1).reshape(-1)
    returned = jnp.take(heating, slot_back, axis=1).reshape(
        levels, band_count, slot_count, block_cols
    )
    home_heat = lax.all_to_all(returned, "band", split_axis=1, concat_axis=1, tiled=True)
    dest_back = (own_start + own_rank) % band_count
    spot_index = dest_back * slot_count + own_rank // band_count
    physics_heat = (
        jnp.take(home_heat.reshape(levels, band_count * slot_count, block_cols), spot_index, axis=1)
        * flag_mask
    )
    physics_heat = physics_heat.reshape(levels, group_size, per_peer)
    dyn_heat = lax.all_to_all(
        physics_heat, "span", split_axis=1, concat_axis=1, tiled=True
    ).reshape(levels, columns)
    return jnp.zeros((levels, columns), jnp.float32).at[:, column_order].set(dyn_heat)


def solution(mesh):
    placed = (
        P(None, None, ("band", "span")),
        P(None, ("band", "span")),
        P(None, ("band", "span")),
        P(("band", "span")),
        P(("band", "span")),
        P(("band", "span")),
        P(("band", "span")),
        P(),
        P(),
    )
    return jax.shard_map(
        local, mesh=mesh, in_specs=placed, out_specs=P(None, ("band", "span")), check_vma=False
    )
```

profile of v0, /device:TPU:1, one launch (start us, length us, event | category | flops | bytes accessed | tf_op | source)
XLA Modules:
  0.0 282.3 jit_solution(17097676135511918596)
XLA Ops:
  3.2 1.3 gather_fusion.1
  5.5 14.5 %all-to-all-start = ((bf16[2,1,32,16]{3,0,1,2:T(2,128)(2,1)}), bf16[2,1,32,16]{3,0,1,2:T(2,128)(2,1)S(1)}, u32[]{:S(2)}, u32[]{:S(2)}) async-start(bf16[2,1,32,16]{3,0,1,2:T(2,128)(2,1)} %broadcast_select_fusion.1), calls=%async_computation | async-start | bytes 32768 | tf_op jit(solution)/shard_map/all_to_all | solution.py:140
  20.0 1.3 dynamic-slice
  22.8 6.8 %all-reduce.2 = s32[32]{0:T(128)S(1)} all-reduce(s32[32]{0:T(128)S(1)} %dynamic-update-slice), channel_id=1, replica_groups=mesh['band'=8,'span'=32] {'band'}, use_global_device_ids=true, to_apply=%add.2 | all-reduce | flops 32 | bytes 256
  32.7 1.9 compare_and_fusion.4
  35.5 1.0 pad_maximum_fusion.2
  36.5 2.0 copy.76
  38.5 2.7 gather_fusion.4
  41.2 1.9 copy.77
  43.6 1.5 reshape.960
  45.1 11.3 %all-to-all-start.2 = ((bf16[32,2,2304]{2,1,0:T(2,128)(2,1)}), bf16[32,2,2304]{2,1,0:T(2,128)(2,1)S(1)}, u32[]{:S(2)}, u32[]{:S(2)}) async-start(bf16[32,2,2304]{2,1,0:T(2,128)(2,1)} %reshape.960), calls=%async_computation.2 | async-start | bytes 589824 | tf_op jit(solution)/shard_map/all_to_all | solution.py:139
  58.5 10.5 %all-to-all-done.2 = bf16[32,2,2304]{2,1,0:T(2,128)(2,1)S(1)} async-done(((bf16[32,2,2304]{2,1,0:T(2,128)(2,1)}), bf16[32,2,2304]{2,1,0:T(2,128)(2,1)S(1)}, u32[]{:S(2)}, u32[]{:S(2)}) %all-to-all-start.2) | async-done | bytes 294944 | tf_op jit(solution)/shard_map/all_to_all | solution.py:139
  69.0 7.7 %all-to-all-start.1 = ((bf16[2,1,8,1,128]{4,0,3,1,2:T(2,128)(2,1)}), bf16[2,1,8,1,128]{4,0,3,1,2:T(2,128)(2,1)S(1)}, u32[]{:S(2)}, u32[]{:S(2)}) async-start(bf16[2,1,8,1,128]{4,0,3,1,2:T(2,128)(2,1)} %fusion.84), calls=%async_computation.1 | async-start | bytes 8192 | tf_op jit(solution)/shard_map/all_to_all | solution.py:166
  79.6 1.9 all-to-all-done.1
  81.5 4.1 %all-to-all-start.3 = ((bf16[9,32,8,1,128]{4,1,0,3,2:T(8,128)(2,1)}), bf16[9,32,8,1,128]{4,1,0,3,2:T(8,128)(2,1)S(1)}, u32[]{:S(2)}, u32[]{:S(2)}) async-start(bf16[9,32,8,1,128]{4,1,0,3,2:T(8,128)(2,1)} %fusion.81), calls=%async_computation.3 | async-start | bytes 1179648 | tf_op jit(solution)/shard_map/all_to_all | solution.py:165
  86.4 15.1 %all-to-all-done.3 = bf16[9,32,8,1,128]{4,1,0,3,2:T(8,128)(2,1)S(1)} async-done(((bf16[9,32,8,1,128]{4,1,0,3,2:T(8,128)(2,1)}), bf16[9,32,8,1,128]{4,1,0,3,2:T(8,128)(2,1)S(1)}, u32[]{:S(2)}, u32[]{:S(2)}) %all-to-all-start.3) | async-done | bytes 589856 | tf_op jit(solution)/shard_map/all_to_all | solution.py:165
  102.2 148.1 %while.85 = (s32[]{:T(128)}, f32[2,32,128]{2,1,0:T(8,128)S(1)}, bf16[2,2,1,128]{3,0,1,2:T(2,128)(2,1)S(1)}, bf16[2,9,32,128]{3,2,1,0:T(8,128)(2,1)S(1)}, bf16[11...) while((s32[]{:T(128)}, f32[2,32,128]{2,1,0:T(8,128)S(1)}, ...), condition=%wide.region_12.13_spmd, body=%wide.region_5.12_spmd.sunk | while | flops 469948672 | bytes 88375600 | solution.py:104
  103.2 5.9 %fusion.127 = f32[32,112,128]{2,1,0:T(8,128)S(1)} fusion(f32[32,128,112,1]{1,2,3,0:T(8,128)S(1)} %fusion.126), kind=kOutput, calls=%fused_computation.191.clone.1 | output fusion | flops 14221312 | bytes 3670016 | tf_op jit(solution)/shard_map/while/body/eval_jaxpr/jit(cumsum)/reduce_window_sum | solution.py:25
  110.4 2.8 bitcast_multiply_fusion.5
  113.2 1.4 broadcast.891.clone
  114.6 1.4 broadcast.891.clone.1
  116.0 14.0 %while.86 = (s32[]{:T(128)}, f32[112,128]{1,0:T(8,128)S(1)}, f32[112,128]{1,0:T(8,128)S(1)}, f32[4,8,112,128]{3,2,1,0:T(8,128)}, f32[4,8,112,128]{3,2,1,0:T(8,12...) while((s32[]{:T(128)}, f32[112,128]{1,0:T(8,128)S(1)}, ...), condition=%wide.region_8.8_spmd, body=%wide.region_7.7_spmd.sunk | while | flops 1290248 | bytes 6136109 | solution.py:58
  116.0 1.4 bitcast_dynamic-update-slice_fusion.53
  118.5 1.0 bitcast_dynamic-update-slice_fusion.69
  119.5 1.4 bitcast_dynamic-update-slice_fusion.53
  122.0 1.0 bitcast_dynamic-update-slice_fusion.69
  123.0 1.4 bitcast_dynamic-update-slice_fusion.53
  125.5 1.0 bitcast_dynamic-update-slice_fusion.69
  126.5 1.4 bitcast_dynamic-update-slice_fusion.53
  129.0 1.0 bitcast_dynamic-update-slice_fusion.69
  130.0 3.5 %fusion.131 = f32[32,112,128]{2,1,0:T(8,128)} fusion(f32[1,112,128]{2,1,0:T(8,128)S(1)} %broadcast_in_dim.228, f32[32,112,128]{2,1,0:T(8,128)} %bitcast.650), kind=kLoop, calls=%fused_computation.184.clone.1 | loop fusion | flops 458752 | bytes 3727360 | tf_op jit(solution)/shard_map/while/body/eval_jaxpr/concatenate | solution.py:68
  134.3 2.9 %fusion.130 = f32[32,112,128]{2,1,0:T(8,128)} fusion(f32[1,112,128]{2,1,0:T(8,128)S(1)} %slice_multiply_fusion.2, f32[32,112,128]{2,1,0:T(8,128)} %bitcast.648), kind=kLoop, calls=%fused_computation.183.clone.1 | loop fusion | flops 458752 | bytes 3727360 | tf_op jit(solution)/shard_map/while/body/eval_jaxpr/concatenate | solution.py:69
  137.1 1.4 broadcast.891
  138.5 34.4 %while.87 = (s32[]{:T(128)}, f32[112,128]{1,0:T(8,128)S(1)}, f32[4,8,112,128]{3,2,1,0:T(8,128)}, f32[4,8,112,128]{3,2,1,0:T(8,128)}, f32[4,8,112,128]{3,2,1,0:T(...) while((s32[]{:T(128)}, f32[112,128]{1,0:T(8,128)S(1)}, ...), condition=%wide.region_10.10_spmd.clone, body=%wide.region_9.9_spmd.clone.sunk | while | flops 817161 | bytes 4588343 | solution.py:85
  138.5 1.1 bitcast_dynamic-update-slice_fusion.70
  139.6 1.0 bitcast_dynamic-update-slice_fusion.71
  141.6 1.0 bitcast_dynamic-update-slice_fusion.73
  148.2 1.0 bitcast_dynamic-update-slice_fusion.71
  158.7 1.0 bitcast_dynamic-update-slice_fusion.73
  172.9 3.2 %fusion.132 = f32[33,112,128]{2,1,0:T(8,128)S(1)} fusion(f32[1,112,128]{2,1,0:T(8,128)S(1)} %slice_multiply_fusion.2, f32[1,112,128]{2,1,0:T(8,128)S(1)} %broadcast_in_dim.228, f32[32,112,128]{2,1,0:T(8,128)} %bitcast.684, f32[32,112,128]{2,1,0:T(8,128)} %bitcast.648, f32[32,112,128]{2,1,0:T(8,128)} %bitcast.650, f32[32,112,128]{2,1,0:T(8,128)S(1)} %copy-done.2, ...), kind=kLoop, calls=%fused_computation.180.clone.1 | loop fusion | flops 4257792 | bytes 9347584 | tf_op jit(solution)/shard_map/while/body/eval_jaxpr/sub | solution.py:97
  177.2 5.9 %fusion.127 = f32[32,112,128]{2,1,0:T(8,128)S(1)} fusion(f32[32,128,112,1]{1,2,3,0:T(8,128)S(1)} %fusion.126), kind=kOutput, calls=%fused_computation.191.clone.1 | output fusion | flops 14221312 | bytes 3670016 | tf_op jit(solution)/shard_map/while/body/eval_jaxpr/jit(cumsum)/reduce_window_sum | solution.py:25
  184.4 2.8 bitcast_multiply_fusion.5
  187.2 1.4 broadcast.891.clone
  188.6 1.4 broadcast.891.clone.1
  190.0 14.0 %while.86 = (s32[]{:T(128)}, f32[112,128]{1,0:T(8,128)S(1)}, f32[112,128]{1,0:T(8,128)S(1)}, f32[4,8,112,128]{3,2,1,0:T(8,128)}, f32[4,8,112,128]{3,2,1,0:T(8,12...) while((s32[]{:T(128)}, f32[112,128]{1,0:T(8,128)S(1)}, ...), condition=%wide.region_8.8_spmd, body=%wide.region_7.7_spmd.sunk | while | flops 1290248 | bytes 6136109 | solution.py:58
  190.0 1.4 bitcast_dynamic-update-slice_fusion.53
  192.5 1.0 bitcast_dynamic-update-slice_fusion.69
  193.5 1.4 bitcast_dynamic-update-slice_fusion.53
  196.0 1.0 bitcast_dynamic-update-slice_fusion.69
  197.0 1.4 bitcast_dynamic-update-slice_fusion.53
  199.5 1.0 bitcast_dynamic-update-slice_fusion.69
  200.5 1.4 bitcast_dynamic-update-slice_fusion.53
  203.0 1.0 bitcast_dynamic-update-slice_fusion.69
  204.0 3.5 %fusion.131 = f32[32,112,128]{2,1,0:T(8,128)} fusion(f32[1,112,128]{2,1,0:T(8,128)S(1)} %broadcast_in_dim.228, f32[32,112,128]{2,1,0:T(8,128)} %bitcast.650), kind=kLoop, calls=%fused_computation.184.clone.1 | loop fusion | flops 458752 | bytes 3727360 | tf_op jit(solution)/shard_map/while/body/eval_jaxpr/concatenate | solution.py:68
  208.3 2.9 %fusion.130 = f32[32,112,128]{2,1,0:T(8,128)} fusion(f32[1,112,128]{2,1,0:T(8,128)S(1)} %slice_multiply_fusion.2, f32[32,112,128]{2,1,0:T(8,128)} %bitcast.648), kind=kLoop, calls=%fused_computation.183.clone.1 | loop fusion | flops 458752 | bytes 3727360 | tf_op jit(solution)/shard_map/while/body/eval_jaxpr/concatenate | solution.py:69
  211.2 1.4 broadcast.891
  212.6 34.4 %while.87 = (s32[]{:T(128)}, f32[112,128]{1,0:T(8,128)S(1)}, f32[4,8,112,128]{3,2,1,0:T(8,128)}, f32[4,8,112,128]{3,2,1,0:T(8,128)}, f32[4,8,112,128]{3,2,1,0:T(...) while((s32[]{:T(128)}, f32[112,128]{1,0:T(8,128)S(1)}, ...), condition=%wide.region_10.10_spmd.clone, body=%wide.region_9.9_spmd.clone.sunk | while | flops 817161 | bytes 4588343 | solution.py:85
  212.6 1.1 bitcast_dynamic-update-slice_fusion.70
  247.0 3.2 %fusion.132 = f32[33,112,128]{2,1,0:T(8,128)S(1)} fusion(f32[1,112,128]{2,1,0:T(8,128)S(1)} %slice_multiply_fusion.2, f32[1,112,128]{2,1,0:T(8,128)S(1)} %broadcast_in_dim.228, f32[32,112,128]{2,1,0:T(8,128)} %bitcast.684, f32[32,112,128]{2,1,0:T(8,128)} %bitcast.648, f32[32,112,128]{2,1,0:T(8,128)} %bitcast.650, f32[32,112,128]{2,1,0:T(8,128)S(1)} %copy-done.2, ...), kind=kLoop, calls=%fused_computation.180.clone.1 | loop fusion | flops 4257792 | bytes 9347584 | tf_op jit(solution)/shard_map/while/body/eval_jaxpr/sub | solution.py:97
  251.6 4.2 %all-to-all-start.4 = ((f32[32,8,1,128]{3,0,2,1:T(8,128)}), f32[32,8,1,128]{3,0,2,1:T(8,128)S(1)}, u32[]{:S(2)}, u32[]{:S(2)}) async-start(f32[32,8,1,128]{3,0,2,1:T(8,128)} %bitcast_select_fusion.1), calls=%async_computation.4 | async-start | bytes 262144 | tf_op jit(solution)/shard_map/all_to_all | solution.py:187
  256.2 5.5 %all-to-all-done.4 = f32[32,8,1,128]{3,0,2,1:T(8,128)S(1)} async-done(((f32[32,8,1,128]{3,0,2,1:T(8,128)}), f32[32,8,1,128]{3,0,2,1:T(8,128)S(1)}, u32[]{:S(2)}, u32[]{:S(2)}) %all-to-all-start.4) | async-done | bytes 131104 | tf_op jit(solution)/shard_map/all_to_all | solution.py:187
  263.3 3.9 %all-to-all-start.5 = ((f32[32,1,512]{2,1,0:T(1,128)}), f32[32,1,512]{2,1,0:T(1,128)S(1)}, u32[]{:S(2)}, u32[]{:S(2)}) async-start(f32[32,1,512]{2,1,0:T(1,128)} %reshape.962), calls=%async_computation.5 | async-start | bytes 131072 | tf_op jit(solution)/shard_map/all_to_all | solution.py:195
  267.2 11.1 %all-to-all-done.5 = f32[32,1,512]{2,1,0:T(1,128)S(1)} async-done(((f32[32,1,512]{2,1,0:T(1,128)}), f32[32,1,512]{2,1,0:T(1,128)S(1)}, u32[]{:S(2)}, u32[]{:S(2)}) %all-to-all-start.5) | async-done | bytes 65568 | tf_op jit(solution)/shard_map/all_to_all | solution.py:195
  279.7 1.8 scatter_custom_fusion
  (317 shorter events, 97.5 us)
Async XLA Ops:
  5.5 39.7 %all-to-all-start = ((bf16[2,1,32,16]{3,0,1,2:T(2,128)(2,1)}), bf16[2,1,32,16]{3,0,1,2:T(2,128)(2,1)S(1)}, u32[]{:S(2)}, u32[]{:S(2)}) async-start(bf16[2,1,32,16]{3,0,1,2:T(2,128)(2,1)} %broadcast_select_fusion.1), calls=%async_computation | async-start | bytes 32768 | tf_op jit(solution)/shard_map/all_to_all | solution.py:140
  45.1 23.9 %all-to-all-start.2 = ((bf16[32,2,2304]{2,1,0:T(2,128)(2,1)}), bf16[32,2,2304]{2,1,0:T(2,128)(2,1)S(1)}, u32[]{:S(2)}, u32[]{:S(2)}) async-start(bf16[32,2,2304]{2,1,0:T(2,128)(2,1)} %reshape.960), calls=%async_computation.2 | async-start | bytes 589824 | tf_op jit(solution)/shard_map/all_to_all | solution.py:139
  69.0 12.5 %all-to-all-start.1 = ((bf16[2,1,8,1,128]{4,0,3,1,2:T(2,128)(2,1)}), bf16[2,1,8,1,128]{4,0,3,1,2:T(2,128)(2,1)S(1)}, u32[]{:S(2)}, u32[]{:S(2)}) async-start(bf16[2,1,8,1,128]{4,0,3,1,2:T(2,128)(2,1)} %fusion.84), calls=%async_computation.1 | async-start | bytes 8192 | tf_op jit(solution)/shard_map/all_to_all | solution.py:166
  78.6 23.6 %copy-start.4 = (bf16[112,60]{0,1:T(8,128)(2,1)S(1)}, bf16[112,60]{0,1:T(8,128)(2,1)}, u32[]{:S(2)}) copy-start(bf16[112,60]{0,1:T(8,128)(2,1)} %param.23) | copy-start | bytes 40324
  78.6 23.6 %copy-start.10 = (bf16[112,7,60]{0,2,1:T(8,128)(2,1)S(1)}, bf16[112,7,60]{0,2,1:T(8,128)(2,1)}, u32[]{:S(2)}) copy-start(bf16[112,7,60]{0,2,1:T(8,128)(2,1)} %param.22) | copy-start | bytes 282244
  81.5 19.9 %all-to-all-start.3 = ((bf16[9,32,8,1,128]{4,1,0,3,2:T(8,128)(2,1)}), bf16[9,32,8,1,128]{4,1,0,3,2:T(8,128)(2,1)S(1)}, u32[]{:S(2)}, u32[]{:S(2)}) async-start(bf16[9,32,8,1,128]{4,1,0,3,2:T(8,128)(2,1)} %fusion.81), calls=%async_computation.3 | async-start | bytes 1179648 | tf_op jit(solution)/shard_map/all_to_all | solution.py:165
  102.2 148.7 %copy-start.6 = (pred[8]{0:T(512)(128)(4,1)S(1)}, pred[8]{0:T(512)(128)(4,1)}, u32[]{:S(2)}) copy-start(pred[8]{0:T(512)(128)(4,1)} %get-tuple-element.492) | copy-start | bytes 28
  102.2 153.7 %copy-start.8 = (s32[4]{0:T(128)S(1)}, s32[4]{0:T(128)}, u32[]{:S(2)}) copy-start(s32[4]{0:T(128)} %param.21) | copy-start | bytes 52
  102.2 153.6 %copy-start.9 = (pred[4]{0:T(512)(128)(4,1)S(1)}, pred[4]{0:T(512)(128)(4,1)}, u32[]{:S(2)}) copy-start(pred[4]{0:T(512)(128)(4,1)} %get-tuple-element.489) | copy-start | bytes 16
  102.2 154.0 %copy-start.7 = (s32[4]{0:T(128)S(1)}, s32[4]{0:T(128)}, u32[]{:S(2)}) copy-start(s32[4]{0:T(128)} %get-tuple-element.490) | copy-start | bytes 52
  109.1 1.2 copy-start.1
  110.4 2.8 copy-start.3
  130.0 3.5 %copy-start = (f32[4,8,112,128]{3,2,1,0:T(8,128)}, f32[4,8,112,128]{3,2,1,0:T(8,128)S(1)}, u32[]{:S(2)}) copy-start(f32[4,8,112,128]{3,2,1,0:T(8,128)S(1)} %get-tuple-element.953) | copy-start | bytes 5505028 | tf_op jit(solution)/shard_map/while
  138.5 34.4 %copy-start.2 = (f32[32,112,128]{2,1,0:T(8,128)S(1)}, f32[32,112,128]{2,1,0:T(8,128)}, u32[]{:S(2)}) copy-start(f32[32,112,128]{2,1,0:T(8,128)} %copy-done.1) | copy-start | bytes 5505028 | tf_op jit(solution)/shard_map/while
  183.2 1.2 copy-start.1
  184.4 2.8 copy-start.3
  204.0 3.5 %copy-start = (f32[4,8,112,128]{3,2,1,0:T(8,128)}, f32[4,8,112,128]{3,2,1,0:T(8,128)S(1)}, u32[]{:S(2)}) copy-start(f32[4,8,112,128]{3,2,1,0:T(8,128)S(1)} %get-tuple-element.953) | copy-start | bytes 5505028 | tf_op jit(solution)/shard_map/while
  212.6 34.4 %copy-start.2 = (f32[32,112,128]{2,1,0:T(8,128)S(1)}, f32[32,112,128]{2,1,0:T(8,128)}, u32[]{:S(2)}) copy-start(f32[32,112,128]{2,1,0:T(8,128)} %copy-done.1) | copy-start | bytes 5505028 | tf_op jit(solution)/shard_map/while
  250.3 16.9 %copy-start.5 = (s32[512]{0:T(512)S(1)}, s32[512]{0:T(512)}, u32[]{:S(2)}) copy-start(s32[512]{0:T(512)} %param.20) | copy-start | bytes 6148
  251.6 10.1 %all-to-all-start.4 = ((f32[32,8,1,128]{3,0,2,1:T(8,128)}), f32[32,8,1,128]{3,0,2,1:T(8,128)S(1)}, u32[]{:S(2)}, u32[]{:S(2)}) async-start(f32[32,8,1,128]{3,0,2,1:T(8,128)} %bitcast_select_fusion.1), calls=%async_computation.4 | async-start | bytes 262144 | tf_op jit(solution)/shard_map/all_to_all | solution.py:187
  263.3 15.0 %all-to-all-start.5 = ((f32[32,1,512]{2,1,0:T(1,128)}), f32[32,1,512]{2,1,0:T(1,128)S(1)}, u32[]{:S(2)}, u32[]{:S(2)}) async-start(f32[32,1,512]{2,1,0:T(1,128)} %reshape.962), calls=%async_computation.5 | async-start | bytes 131072 | tf_op jit(solution)/shard_map/all_to_all | solution.py:195
where the time goes:
time: 288 us; the launch traced here: 282 us
  other arithmetic  125 us (43%)
  local copies, waits for them, and re-layouts  51.3 us (18%)
  starting transfers between devices  45.7 us (16%)
  waiting for transfers between devices  44 us (15%)
  matrix products  7 us (2%)
  blocking collectives  6.82 us (2%)
    while x74, other arithmetic  72.5 us
    all_to_all x1, waiting for transfers between devices, local(): lax.all_to_all(send_fields, 'band', split_axis=2, concat_axis=2, tiled=True)  15.1 us
    dynamic_update_slice x16, local copies, waits for them, and re-layouts, column_heating(): lax.scan(upward, (floor_refl, floor_source), (reflect.reshape(grouped_sha...  14.5 us
    all_to_all x1, starting transfers between devices, local(): lax.all_to_all(ground, 'span', split_axis=2, concat_axis=2, tiled=True)  14.5 us
    another operation x2, other arithmetic, column_heating(): column_path = jnp.cumsum(optical_depth, axis=0)  11.9 us
    all_to_all x1, starting transfers between devices, local(): lax.all_to_all(fields, 'span', split_axis=2, concat_axis=2, tiled=True)  11.3 us
    all_to_all x1, waiting for transfers between devices, local(): lax.all_to_all(physics_heat, 'span', split_axis=1, concat_axis=1, tiled=T...  11.1 us
    all_to_all x1, waiting for transfers between devices, local(): lax.all_to_all(fields, 'span', split_axis=2, concat_axis=2, tiled=True)  10.5 us
  transfers between devices with their start and end apart: 6, of which 5 were waited for; matrix products, arithmetic and copies ran while one was open for 8% of the time, Pallas kernels for 0%

commit v1 on v0

--- a/solution.py
+++ b/solution.py
@@ -2,6 +2,12 @@
 import jax.numpy as jnp
 from jax import lax
 from jax.sharding import PartitionSpec as P
+
+
+def exchange_blocks(array, mesh_axis, split, join):
+    cells = jnp.split(array, lax.axis_size(mesh_axis), axis=split)
+    received = lax.all_to_all(jnp.stack(cells), mesh_axis, 0, 0)
+    return jnp.concatenate(received, axis=join)
 
 
 def column_heating(profile, ground_pair, absorption, scattering):
@@ -162,7 +168,7 @@
     )
     send_ground = jnp.take(ground, chosen, axis=2).reshape(2, 1, band_count, slot_count, block_cols)
     got_fields, got_ground = (
-        lax.all_to_all(send_fields, "band", split_axis=2, concat_axis=2, tiled=True),
+        exchange_blocks(send_fields, "band", 2, 2),
         lax.all_to_all(send_ground, "band", split_axis=2, concat_axis=2, tiled=True),
     )
     work_rank = jnp.arange(working, dtype=jnp.int32) * band_count + me_band

time: 288 us -> 291 us (1.010)
  local copies, waits for them, and re-layouts: 51.3 us -> 56.3 us
    unnamed x21 -> x28, local copies, waits for them, and re-layouts: 5.27 us -> 9.66 us
    all_to_all x1, starting transfers between devices: 14.5 us -> 11 us  [local(): lax.all_to_all(ground, 'span', split_axis=2, concat_axis=2, tiled=True)]
    another operation x6 -> x7, local copies, waits for them, and re-layouts: 8.43 us -> 8.97 us
  transfers between devices with their start and end apart: 6 -> 6, of which waited for: 5 -> 4; matrix products, arithmetic and copies ran while one was open for 8% -> 9% of each run, Pallas kernels for 0% -> 0%
where the time goes in v1:
time: 291 us; the launch traced here: 285 us
  other arithmetic  124 us (43%)
  local copies, waits for them, and re-layouts  56.3 us (19%)
  starting transfers between devices  43.8 us (15%)
  waiting for transfers between devices  42.1 us (14%)
  blocking collectives  9.46 us (3%)
  matrix products  7.01 us (2%)
    while x74, other arithmetic  72.5 us
    dynamic_update_slice x16, local copies, waits for them, and re-layouts, column_heating(): lax.scan(upward, (floor_refl, floor_source), (reflect.reshape(grouped_sha...  14.6 us
    all_to_all x1, waiting for transfers between devices, exchange_blocks(): received = lax.all_to_all(jnp.stack(cells), mesh_axis, 0, 0)  14.4 us
    another operation x2, other arithmetic, column_heating(): column_path = jnp.cumsum(optical_depth, axis=0)  11.9 us
    all_to_all x1, starting transfers between devices, local(): lax.all_to_all(fields, 'span', split_axis=2, concat_axis=2, tiled=True)  11.6 us
    all_to_all x1, waiting for transfers between devices, local(): lax.all_to_all(fields, 'span', split_axis=2, concat_axis=2, tiled=True)  11.1 us
    all_to_all x1, waiting for transfers between devices, local(): lax.all_to_all(physics_heat, 'span', split_axis=1, concat_axis=1, tiled=T...  11.1 us
    all_to_all x1, starting transfers between devices, local(): lax.all_to_all(ground, 'span', split_axis=2, concat_axis=2, tiled=True)  11 us
  transfers between devices with their start and end apart: 6, of which 4 were waited for; matrix products, arithmetic and copies ran while one was open for 9% of the time, Pallas kernels for 0%

profile of v1, /device:TPU:1, one launch (start us, length us, event | category | flops | bytes accessed | tf_op | source)
XLA Modules:
  0.0 285.4 jit_solution(2632677584849667960)
XLA Ops:
  1.5 1.3 dynamic-slice
  4.3 9.5 %all-reduce.2 = s32[32]{0:T(128)S(1)} all-reduce(s32[32]{0:T(128)S(1)} %dynamic-update-slice), channel_id=1, replica_groups=mesh['band'=8,'span'=32] {'band'}, use_global_device_ids=true, to_apply=%add.2 | all-reduce | flops 32 | bytes 256
  16.0 1.3 gather_fusion.1
  18.3 11.0 %all-to-all-start = ((bf16[2,1,32,16]{3,0,1,2:T(2,128)(2,1)}), bf16[2,1,32,16]{3,0,1,2:T(2,128)(2,1)S(1)}, u32[]{:S(2)}, u32[]{:S(2)}) async-start(bf16[2,1,32,16]{3,0,1,2:T(2,128)(2,1)} %broadcast_select_fusion.1), calls=%async_computation | async-start | bytes 32768 | tf_op jit(solution)/shard_map/all_to_all | solution.py:146
  32.0 1.8 compare_and_fusion.4
  34.6 1.0 pad_maximum_fusion.2
  35.6 2.0 copy.102
  37.6 2.7 gather_fusion.4
  40.4 1.9 copy.103
  42.7 1.5 reshape.960
  44.2 11.6 %all-to-all-start.2 = ((bf16[32,2,2304]{2,1,0:T(2,128)(2,1)}), bf16[32,2,2304]{2,1,0:T(2,128)(2,1)S(1)}, u32[]{:S(2)}, u32[]{:S(2)}) async-start(bf16[32,2,2304]{2,1,0:T(2,128)(2,1)} %reshape.960), calls=%async_computation.2 | async-start | bytes 589824 | tf_op jit(solution)/shard_map/all_to_all | solution.py:145
  57.2 11.1 %all-to-all-done.2 = bf16[32,2,2304]{2,1,0:T(2,128)(2,1)S(1)} async-done(((bf16[32,2,2304]{2,1,0:T(2,128)(2,1)}), bf16[32,2,2304]{2,1,0:T(2,128)(2,1)S(1)}, u32[]{:S(2)}, u32[]{:S(2)}) %all-to-all-start.2) | async-done | bytes 294944 | tf_op jit(solution)/shard_map/all_to_all | solution.py:145
  68.4 8.0 %all-to-all-start.1 = ((bf16[2,1,8,1,128]{4,0,3,1,2:T(2,128)(2,1)}), bf16[2,1,8,1,128]{4,0,3,1,2:T(2,128)(2,1)S(1)}, u32[]{:S(2)}, u32[]{:S(2)}) async-start(bf16[2,1,8,1,128]{4,0,3,1,2:T(2,128)(2,1)} %fusion.91), calls=%async_computation.1 | async-start | bytes 8192 | tf_op jit(solution)/shard_map/all_to_all | solution.py:172
  83.7 5.1 %all-to-all-start.3 = ((bf16[8,9,32,1,1,128]{5,2,1,4,3,0:T(8,128)(2,1)}), bf16[8,9,32,1,1,128]{5,2,1,4,3,0:T(8,128)(2,1)S(1)}, u32[]{:S(2)}, u32[]{:S(2)}) async-start(bf16[8,9,32,1,1,128]{5,2,1,4,3,0:T(8,128)(2,1)} %fusion.83), calls=%async_computation.3 | async-start | bytes 1179648 | tf_op jit(solution)/shard_map/all_to_all | solution.py:9
  90.2 14.4 %all-to-all-done.3 = bf16[8,9,32,1,1,128]{5,2,1,4,3,0:T(8,128)(2,1)S(1)} async-done(((bf16[8,9,32,1,1,128]{5,2,1,4,3,0:T(8,128)(2,1)}), bf16[8,9,32,1,1,128]{5,2,1,4,3,0:T(8,128)(2,1)S(1)}, u32[]{:S(2)}, u32[]{:S(2)}) %all-to-all-start.3) | async-done | bytes 589856 | tf_op jit(solution)/shard_map/all_to_all | solution.py:9
  105.3 148.1 %while.85 = (s32[]{:T(128)}, f32[2,32,128]{2,1,0:T(8,128)S(1)}, bf16[2,2,1,128]{3,0,1,2:T(2,128)(2,1)S(1)}, bf16[2,9,32,128]{3,2,1,0:T(8,128)(2,1)S(1)}, bf16[11...) while((s32[]{:T(128)}, f32[2,32,128]{2,1,0:T(8,128)S(1)}, ...), condition=%wide.region_12.13_spmd, body=%wide.region_5.12_spmd.sunk | while | flops 469948672 | bytes 88375600 | solution.py:110
  106.3 5.9 %fusion.135 = f32[32,112,128]{2,1,0:T(8,128)S(1)} fusion(f32[32,128,112,1]{1,2,3,0:T(8,128)S(1)} %fusion.134), kind=kOutput, calls=%fused_computation.191.clone.1 | output fusion | flops 14221312 | bytes 3670016 | tf_op jit(solution)/shard_map/while/body/eval_jaxpr/jit(cumsum)/reduce_window_sum | solution.py:31
  113.4 2.8 bitcast_multiply_fusion.5
  116.2 1.4 broadcast.891.clone
  117.7 1.4 broadcast.891.clone.1
  119.0 14.0 %while.86 = (s32[]{:T(128)}, f32[112,128]{1,0:T(8,128)S(1)}, f32[112,128]{1,0:T(8,128)S(1)}, f32[4,8,112,128]{3,2,1,0:T(8,128)}, f32[4,8,112,128]{3,2,1,0:T(8,12...) while((s32[]{:T(128)}, f32[112,128]{1,0:T(8,128)S(1)}, ...), condition=%wide.region_8.8_spmd, body=%wide.region_7.7_spmd.sunk | while | flops 1290248 | bytes 6136109 | solution.py:64
  119.0 1.4 bitcast_dynamic-update-slice_fusion.53
  121.5 1.0 bitcast_dynamic-update-slice_fusion.69
  122.5 1.4 bitcast_dynamic-update-slice_fusion.53
  125.0 1.0 bitcast_dynamic-update-slice_fusion.69
  126.0 1.4 bitcast_dynamic-update-slice_fusion.53
  128.5 1.0 bitcast_dynamic-update-slice_fusion.69
  129.5 1.4 bitcast_dynamic-update-slice_fusion.53
  132.0 1.0 bitcast_dynamic-update-slice_fusion.69
  133.0 3.5 %fusion.139 = f32[32,112,128]{2,1,0:T(8,128)} fusion(f32[1,112,128]{2,1,0:T(8,128)S(1)} %broadcast_in_dim.232, f32[32,112,128]{2,1,0:T(8,128)} %bitcast.687), kind=kLoop, calls=%fused_computation.184.clone.1 | loop fusion | flops 458752 | bytes 3727360 | tf_op jit(solution)/shard_map/while/body/eval_jaxpr/concatenate | solution.py:74
  137.3 2.9 %fusion.138 = f32[32,112,128]{2,1,0:T(8,128)} fusion(f32[1,112,128]{2,1,0:T(8,128)S(1)} %slice_multiply_fusion.2, f32[32,112,128]{2,1,0:T(8,128)} %bitcast.685), kind=kLoop, calls=%fused_computation.183.clone.1 | loop fusion | flops 458752 | bytes 3727360 | tf_op jit(solution)/shard_map/while/body/eval_jaxpr/concatenate | solution.py:75
  140.2 1.4 broadcast.891
  141.6 34.4 %while.87 = (s32[]{:T(128)}, f32[112,128]{1,0:T(8,128)S(1)}, f32[4,8,112,128]{3,2,1,0:T(8,128)}, f32[4,8,112,128]{3,2,1,0:T(8,128)}, f32[4,8,112,128]{3,2,1,0:T(...) while((s32[]{:T(128)}, f32[112,128]{1,0:T(8,128)S(1)}, ...), condition=%wide.region_10.10_spmd.clone, body=%wide.region_9.9_spmd.clone.sunk | while | flops 817161 | bytes 4588343 | solution.py:91
  141.6 1.1 bitcast_dynamic-update-slice_fusion.70
  144.6 1.0 bitcast_dynamic-update-slice_fusion.73
  153.2 1.0 bitcast_dynamic-update-slice_fusion.73
  161.8 1.0 bitcast_dynamic-update-slice_fusion.73
  172.3 1.0 bitcast_dynamic-update-slice_fusion.75
  176.0 3.2 %fusion.140 = f32[33,112,128]{2,1,0:T(8,128)S(1)} fusion(f32[1,112,128]{2,1,0:T(8,128)S(1)} %slice_multiply_fusion.2, f32[1,112,128]{2,1,0:T(8,128)S(1)} %broadcast_in_dim.232, f32[32,112,128]{2,1,0:T(8,128)} %bitcast.721, f32[32,112,128]{2,1,0:T(8,128)} %bitcast.685, f32[32,112,128]{2,1,0:T(8,128)} %bitcast.687, f32[32,112,128]{2,1,0:T(8,128)S(1)} %copy-done.2, ...), kind=kLoop, calls=%fused_computation.180.clone.1 | loop fusion | flops 4257792 | bytes 9347584 | tf_op jit(solution)/shard_map/while/body/eval_jaxpr/sub | solution.py:103
  180.3 5.9 %fusion.135 = f32[32,112,128]{2,1,0:T(8,128)S(1)} fusion(f32[32,128,112,1]{1,2,3,0:T(8,128)S(1)} %fusion.134), kind=kOutput, calls=%fused_computation.191.clone.1 | output fusion | flops 14221312 | bytes 3670016 | tf_op jit(solution)/shard_map/while/body/eval_jaxpr/jit(cumsum)/reduce_window_sum | solution.py:31
  187.5 2.8 bitcast_multiply_fusion.5
  190.3 1.4 broadcast.891.clone
  191.7 1.4 broadcast.891.clone.1
  193.1 14.0 %while.86 = (s32[]{:T(128)}, f32[112,128]{1,0:T(8,128)S(1)}, f32[112,128]{1,0:T(8,128)S(1)}, f32[4,8,112,128]{3,2,1,0:T(8,128)}, f32[4,8,112,128]{3,2,1,0:T(8,12...) while((s32[]{:T(128)}, f32[112,128]{1,0:T(8,128)S(1)}, ...), condition=%wide.region_8.8_spmd, body=%wide.region_7.7_spmd.sunk | while | flops 1290248 | bytes 6136109 | solution.py:64
  193.1 1.4 bitcast_dynamic-update-slice_fusion.53
  195.6 1.0 bitcast_dynamic-update-slice_fusion.69
  196.6 1.4 bitcast_dynamic-update-slice_fusion.53
  199.1 1.0 bitcast_dynamic-update-slice_fusion.69
  200.1 1.4 bitcast_dynamic-update-slice_fusion.53
  202.5 1.0 bitcast_dynamic-update-slice_fusion.69
  203.6 1.4 bitcast_dynamic-update-slice_fusion.53
  206.0 1.0 bitcast_dynamic-update-slice_fusion.69
  207.1 3.5 %fusion.139 = f32[32,112,128]{2,1,0:T(8,128)} fusion(f32[1,112,128]{2,1,0:T(8,128)S(1)} %broadcast_in_dim.232, f32[32,112,128]{2,1,0:T(8,128)} %bitcast.687), kind=kLoop, calls=%fused_computation.184.clone.1 | loop fusion | flops 458752 | bytes 3727360 | tf_op jit(solution)/shard_map/while/body/eval_jaxpr/concatenate | solution.py:74
  211.4 2.9 %fusion.138 = f32[32,112,128]{2,1,0:T(8,128)} fusion(f32[1,112,128]{2,1,0:T(8,128)S(1)} %slice_multiply_fusion.2, f32[32,112,128]{2,1,0:T(8,128)} %bitcast.685), kind=kLoop, calls=%fused_computation.183.clone.1 | loop fusion | flops 458752 | bytes 3727360 | tf_op jit(solution)/shard_map/while/body/eval_jaxpr/concatenate | solution.py:75
  214.3 1.4 broadcast.891
  215.6 34.4 %while.87 = (s32[]{:T(128)}, f32[112,128]{1,0:T(8,128)S(1)}, f32[4,8,112,128]{3,2,1,0:T(8,128)}, f32[4,8,112,128]{3,2,1,0:T(8,128)}, f32[4,8,112,128]{3,2,1,0:T(...) while((s32[]{:T(128)}, f32[112,128]{1,0:T(8,128)S(1)}, ...), condition=%wide.region_10.10_spmd.clone, body=%wide.region_9.9_spmd.clone.sunk | while | flops 817161 | bytes 4588343 | solution.py:91
  215.6 1.1 bitcast_dynamic-update-slice_fusion.70
  220.6 1.0 bitcast_dynamic-update-slice_fusion.75
  250.1 3.2 %fusion.140 = f32[33,112,128]{2,1,0:T(8,128)S(1)} fusion(f32[1,112,128]{2,1,0:T(8,128)S(1)} %slice_multiply_fusion.2, f32[1,112,128]{2,1,0:T(8,128)S(1)} %broadcast_in_dim.232, f32[32,112,128]{2,1,0:T(8,128)} %bitcast.721, f32[32,112,128]{2,1,0:T(8,128)} %bitcast.685, f32[32,112,128]{2,1,0:T(8,128)} %bitcast.687, f32[32,112,128]{2,1,0:T(8,128)S(1)} %copy-done.2, ...), kind=kLoop, calls=%fused_computation.180.clone.1 | loop fusion | flops 4257792 | bytes 9347584 | tf_op jit(solution)/shard_map/while/body/eval_jaxpr/sub | solution.py:103
  254.7 4.2 %all-to-all-start.4 = ((f32[32,8,1,128]{3,0,2,1:T(8,128)}), f32[32,8,1,128]{3,0,2,1:T(8,128)S(1)}, u32[]{:S(2)}, u32[]{:S(2)}) async-start(f32[32,8,1,128]{3,0,2,1:T(8,128)} %bitcast_select_fusion.1), calls=%async_computation.4 | async-start | bytes 262144 | tf_op jit(solution)/shard_map/all_to_all | solution.py:193
  259.3 5.5 %all-to-all-done.4 = f32[32,8,1,128]{3,0,2,1:T(8,128)S(1)} async-done(((f32[32,8,1,128]{3,0,2,1:T(8,128)}), f32[32,8,1,128]{3,0,2,1:T(8,128)S(1)}, u32[]{:S(2)}, u32[]{:S(2)}) %all-to-all-start.4) | async-done | bytes 131104 | tf_op jit(solution)/shard_map/all_to_all | solution.py:193
  266.4 3.9 %all-to-all-start.5 = ((f32[32,1,512]{2,1,0:T(1,128)}), f32[32,1,512]{2,1,0:T(1,128)S(1)}, u32[]{:S(2)}, u32[]{:S(2)}) async-start(f32[32,1,512]{2,1,0:T(1,128)} %reshape.962), calls=%async_computation.5 | async-start | bytes 131072 | tf_op jit(solution)/shard_map/all_to_all | solution.py:201
  270.3 11.1 %all-to-all-done.5 = f32[32,1,512]{2,1,0:T(1,128)S(1)} async-done(((f32[32,1,512]{2,1,0:T(1,128)}), f32[32,1,512]{2,1,0:T(1,128)S(1)}, u32[]{:S(2)}, u32[]{:S(2)}) %all-to-all-start.5) | async-done | bytes 65568 | tf_op jit(solution)/shard_map/all_to_all | solution.py:201
  282.9 1.8 scatter_custom_fusion
  (323 shorter events, 100.9 us)
Async XLA Ops:
  18.3 25.9 %all-to-all-start = ((bf16[2,1,32,16]{3,0,1,2:T(2,128)(2,1)}), bf16[2,1,32,16]{3,0,1,2:T(2,128)(2,1)S(1)}, u32[]{:S(2)}, u32[]{:S(2)}) async-start(bf16[2,1,32,16]{3,0,1,2:T(2,128)(2,1)} %broadcast_select_fusion.1), calls=%async_computation | async-start | bytes 32768 | tf_op jit(solution)/shard_map/all_to_all | solution.py:146
  44.2 24.2 %all-to-all-start.2 = ((bf16[32,2,2304]{2,1,0:T(2,128)(2,1)}), bf16[32,2,2304]{2,1,0:T(2,128)(2,1)S(1)}, u32[]{:S(2)}, u32[]{:S(2)}) async-start(bf16[32,2,2304]{2,1,0:T(2,128)(2,1)} %reshape.960), calls=%async_computation.2 | async-start | bytes 589824 | tf_op jit(solution)/shard_map/all_to_all | solution.py:145
  68.4 15.3 %all-to-all-start.1 = ((bf16[2,1,8,1,128]{4,0,3,1,2:T(2,128)(2,1)}), bf16[2,1,8,1,128]{4,0,3,1,2:T(2,128)(2,1)S(1)}, u32[]{:S(2)}, u32[]{:S(2)}) async-start(bf16[2,1,8,1,128]{4,0,3,1,2:T(2,128)(2,1)} %fusion.91), calls=%async_computation.1 | async-start | bytes 8192 | tf_op jit(solution)/shard_map/all_to_all | solution.py:172
  78.6 26.7 %copy-start.4 = (bf16[112,60]{0,1:T(8,128)(2,1)S(1)}, bf16[112,60]{0,1:T(8,128)(2,1)}, u32[]{:S(2)}) copy-start(bf16[112,60]{0,1:T(8,128)(2,1)} %param.23) | copy-start | bytes 40324
  78.6 26.7 %copy-start.10 = (bf16[112,7,60]{0,2,1:T(8,128)(2,1)S(1)}, bf16[112,7,60]{0,2,1:T(8,128)(2,1)}, u32[]{:S(2)}) copy-start(bf16[112,7,60]{0,2,1:T(8,128)(2,1)} %param.22) | copy-start | bytes 282244
  83.7 20.9 %all-to-all-start.3 = ((bf16[8,9,32,1,1,128]{5,2,1,4,3,0:T(8,128)(2,1)}), bf16[8,9,32,1,1,128]{5,2,1,4,3,0:T(8,128)(2,1)S(1)}, u32[]{:S(2)}, u32[]{:S(2)}) async-start(bf16[8,9,32,1,1,128]{5,2,1,4,3,0:T(8,128)(2,1)} %fusion.83), calls=%async_computation.3 | async-start | bytes 1179648 | tf_op jit(solution)/shard_map/all_to_all | solution.py:9
  105.3 148.7 %copy-start.6 = (pred[8]{0:T(512)(128)(4,1)S(1)}, pred[8]{0:T(512)(128)(4,1)}, u32[]{:S(2)}) copy-start(pred[8]{0:T(512)(128)(4,1)} %get-tuple-element.492) | copy-start | bytes 28
  105.3 153.7 %copy-start.8 = (s32[4]{0:T(128)S(1)}, s32[4]{0:T(128)}, u32[]{:S(2)}) copy-start(s32[4]{0:T(128)} %param.21) | copy-start | bytes 52
  105.3 153.7 %copy-start.9 = (pred[4]{0:T(512)(128)(4,1)S(1)}, pred[4]{0:T(512)(128)(4,1)}, u32[]{:S(2)}) copy-start(pred[4]{0:T(512)(128)(4,1)} %get-tuple-element.489) | copy-start | bytes 16
  105.3 154.0 %copy-start.7 = (s32[4]{0:T(128)S(1)}, s32[4]{0:T(128)}, u32[]{:S(2)}) copy-start(s32[4]{0:T(128)} %get-tuple-element.490) | copy-start | bytes 52
  112.2 1.2 copy-start.1
  113.4 2.8 copy-start.3
  133.0 3.5 %copy-start = (f32[4,8,112,128]{3,2,1,0:T(8,128)}, f32[4,8,112,128]{3,2,1,0:T(8,128)S(1)}, u32[]{:S(2)}) copy-start(f32[4,8,112,128]{3,2,1,0:T(8,128)S(1)} %get-tuple-element.957) | copy-start | bytes 5505028 | tf_op jit(solution)/shard_map/while
  141.6 34.4 %copy-start.2 = (f32[32,112,128]{2,1,0:T(8,128)S(1)}, f32[32,112,128]{2,1,0:T(8,128)}, u32[]{:S(2)}) copy-start(f32[32,112,128]{2,1,0:T(8,128)} %copy-done.1) | copy-start | bytes 5505028 | tf_op jit(solution)/shard_map/while
  186.3 1.2 copy-start.1
  187.5 2.8 copy-start.3
  207.0 3.5 %copy-start = (f32[4,8,112,128]{3,2,1,0:T(8,128)}, f32[4,8,112,128]{3,2,1,0:T(8,128)S(1)}, u32[]{:S(2)}) copy-start(f32[4,8,112,128]{3,2,1,0:T(8,128)S(1)} %get-tuple-element.957) | copy-start | bytes 5505028 | tf_op jit(solution)/shard_map/while
  215.6 34.4 %copy-start.2 = (f32[32,112,128]{2,1,0:T(8,128)S(1)}, f32[32,112,128]{2,1,0:T(8,128)}, u32[]{:S(2)}) copy-start(f32[32,112,128]{2,1,0:T(8,128)} %copy-done.1) | copy-start | bytes 5505028 | tf_op jit(solution)/shard_map/while
  253.4 16.9 %copy-start.5 = (s32[512]{0:T(512)S(1)}, s32[512]{0:T(512)}, u32[]{:S(2)}) copy-start(s32[512]{0:T(512)} %param.20) | copy-start | bytes 6148
  254.7 10.1 %all-to-all-start.4 = ((f32[32,8,1,128]{3,0,2,1:T(8,128)}), f32[32,8,1,128]{3,0,2,1:T(8,128)S(1)}, u32[]{:S(2)}, u32[]{:S(2)}) async-start(f32[32,8,1,128]{3,0,2,1:T(8,128)} %bitcast_select_fusion.1), calls=%async_computation.4 | async-start | bytes 262144 | tf_op jit(solution)/shard_map/all_to_all | solution.py:193
  266.4 15.0 %all-to-all-start.5 = ((f32[32,1,512]{2,1,0:T(1,128)}), f32[32,1,512]{2,1,0:T(1,128)S(1)}, u32[]{:S(2)}, u32[]{:S(2)}) async-start(f32[32,1,512]{2,1,0:T(1,128)} %reshape.962), calls=%async_computation.5 | async-start | bytes 131072 | tf_op jit(solution)/shard_map/all_to_all | solution.py:201
